TPU v7x, 32 devices: a whole 2x2x4 slice. The times are simulated.
32 devices in a mesh: req: 8 (over y, x, core), mp: 4 (over z).
Axes of the slice: x: 2, y: 2, z: 4, core: 2. Of those that a mesh axis runs over, the one named last changes fastest.
Arguments:
- latents: bfloat16 [16, 1, 384, 416], P('req', None, 'mp'), may hold values from -12 to 12
- prior_frame_cache: bfloat16 [16, 2, 384, 416], P('req', None, 'mp'), may hold values from -6 to 6
- move_to: int32 [16], P('req'), may hold values from 0 to 15, as said below
- counts: int32 [8], P('req'), may hold values from 1 to 2, as said below
- norm_gain: bfloat16 [384], P('mp'), may hold values from 0.5 to 1.5
- conv_weight: bfloat16 [27, 384, 384], P(None, 'mp'), may hold values from -0.0625 to 0.0625
- conv_bias: float32 [384], P('mp'), may hold values from -1.5 to 1.5
Outputs:
- decoded: bfloat16 [16, 1, 384, 416], P('req', None, 'mp')
- new_cache: bfloat16 [16, 2, 384, 416], P('req', None, 'mp')
Inputs may be any that keep to these rules, and one draw needn't show every extreme that they name: move_to is a permutation of the slots; a stream's new slot lies on its old index of req or on the next or previous one, the last and first index being neighbours; every index hands exactly 1 stream to each neighbour and takes the same number back from it. `counts`: some index of req is full and some other holds a single stream.
All inputs are finite; a program needn't handle non-finite values.
Results may differ from a plain program's by a relative error of at most 0.0018.
Values may be sent and summed in bfloat16 or wider, within the bound.
A program may use at most 64 MiB of HBM per device.

v0:
```python
import jax
import jax.numpy as jnp
from jax import lax
from jax.sharding import PartitionSpec as P

SECTION_CHANNELS = 384
LATENT_COLUMNS = 104


def shifted_2(block, axis, distance):
    devices = range(lax.axis_size(axis))
    route = [((i - distance) % len(devices), i) for i in devices]
    return lax.ppermute(block, axis, route)


def apply_taps(running, shard_in, weights, row_width):
    frames = shard_in.shape[1] - 2
    pixels = shard_in.shape[3]
    padded = jnp.pad(shard_in, ((0, 0), (0, 0), (0, 0), (row_width + 1, row_width + 1)))
    column = jnp.arange(pixels + 2 * row_width) % row_width
    for step_x in range(3):
        inside = ((column + step_x - 1 >= 0) & (column + step_x - 1 < row_width)).astype(
            shard_in.dtype
        )
        shifted = padded[:, :, :, step_x : step_x + pixels + 2 * row_width] * inside
        for step_y in range(3):
            window = shifted[:, :, :, step_y * row_width : step_y * row_width + pixels]
            for step_t in range(3):
                running = running + jnp.einsum(
                    "oc,stcp->stop",
                    weights[step_t * 9 + step_y * 3 + step_x],
                    window[:, step_t : step_t + frames],
                    preferred_element_type=jnp.float32,
                )
    return running


def pack_slots(prior_frame_cache, chosen, target, capacity):
    ranking = jnp.cumsum(chosen.astype(jnp.int32)) - 1
    picker = (chosen[None, :] & (ranking[None, :] == jnp.arange(capacity)[:, None])).astype(
        jnp.bfloat16
    )
    blocks = jnp.einsum(
        "cs,sfkp->cfkp", picker, prior_frame_cache, preferred_element_type=jnp.float32
    ).astype(jnp.bfloat16)
    labels = (jnp.dot(picker.astype(jnp.float32), (target + 1).astype(jnp.float32)) - 1.0).astype(
        jnp.bfloat16
    )
    return (blocks, labels)


def migrate(prior_frame_cache, move_to):
    slot_count = prior_frame_cache.shape[0]
    member_slots = lax.axis_size("req")
    position = lax.axis_index("req")
    capacity = slot_count // 2
    device = move_to // slot_count
    target = move_to % slot_count
    offset = (device - position) % member_slots
    goes_right = offset == 1
    goes_left = offset == member_slots - 1
    stays_put = offset == 0
    blocks_right, labels_right = pack_slots(prior_frame_cache, goes_right, target, capacity)
    blocks_left, labels_left = pack_slots(prior_frame_cache, goes_left, target, capacity)
    from_left = shifted_2((blocks_right, labels_right), "req", 1)
    from_right = shifted_2((blocks_left, labels_left), "req", -1)
    sources = jnp.concatenate([prior_frame_cache, from_left[0], from_right[0]], axis=0)
    own_labels = jnp.where(stays_put, target, -1).astype(jnp.float32)
    labels = jnp.concatenate(
        [own_labels, from_left[1].astype(jnp.float32), from_right[1].astype(jnp.float32)]
    )
    placing = (labels[None, :] == jnp.arange(slot_count, dtype=jnp.float32)[:, None]).astype(
        jnp.bfloat16
    )
    return jnp.einsum("ns,sfkp->nfkp", placing, sources, preferred_element_type=jnp.float32).astype(
        jnp.bfloat16
    )


def normalize(values, squares, gains):
    scaled = (
        values.astype(jnp.float32)
        * lax.rsqrt(squares / SECTION_CHANNELS + 1e-06)
        * gains.astype(jnp.float32)[:, None]
    )
    return jax.nn.silu(scaled).astype(jnp.bfloat16)


def shards(latents, prior_frame_cache, move_to, counts, norm_gain, conv_weight, conv_bias):
    moved = migrate(prior_frame_cache, move_to)
    slot_count = latents.shape[0]
    frames = latents.shape[1]
    live = (jnp.arange(slot_count) < counts[0])[:, None, None, None]
    start_zero = jnp.zeros(
        (slot_count, frames, conv_weight.shape[1], latents.shape[3]), jnp.float32
    )
    values = latents.astype(jnp.float32)
    partial_squares = jnp.sum(values * values, axis=2, keepdims=True)
    squares = lax.psum(partial_squares, "mp")
    hidden = normalize(latents, squares, norm_gain)
    extended = jnp.concatenate([moved, hidden], axis=1)
    conv_sum = apply_taps(
        start_zero, lax.all_gather(extended, "mp", axis=2, tiled=True), conv_weight, LATENT_COLUMNS
    )
    total = latents.astype(jnp.float32) + conv_sum + conv_bias[:, None]
    decoded = jnp.where(live, total, jnp.zeros_like(total)).astype(jnp.bfloat16)
    new_cache = extended[:, frames:]
    return (decoded, new_cache)


def solution(mesh):
    in_specs = (
        P("req", None, "mp", None),
        P("req", None, "mp", None),
        P("req"),
        P("req"),
        P("mp"),
        P(None, "mp", None),
        P("mp"),
    )
    out_specs = (P("req", None, "mp", None), P("req", None, "mp", None))
    return jax.shard_map(shards, mesh=mesh, in_specs=in_specs, out_specs=out_specs, check_vma=False)
```

profile of v0, /device:TPU:0, one launch (start us, length us, event | category | flops | bytes accessed | tf_op | source)
XLA Modules:
  0.0 157.5 jit_solution(8122907851598073962)
XLA Ops:
  7.2 0.7 fusion.140
  8.3 0.6 select_reduce_fusion.1
  9.5 1.5 collective-permute-start
  11.7 4.0 %collective-permute-start.1 = (bf16[1]{0:T(256)(128)(2,1)}, bf16[1]{0:T(256)(128)(2,1)}, u32[]{:S(2)}, u32[]{:S(2)}) collective-permute-start(bf16[1]{0:T(256)(128)(2,1)} %bitcast.7), channel_id=1, source_target_pairs={{4,0},{8,4},{12,8},{16,12},{20,16},{24,20},{28,24},{0,28},{5,1},{9... | collective-permute-start | bytes 14 | tf_op jit(solution)/shard_map/ppermute | solution.py:13
  15.7 1.4 copy.130
  17.1 0.6 fusion.135
  17.7 0.3 copy.128
  18.1 0.6 fusion.133
  18.7 0.3 copy.129
  19.0 2.7 %collective-permute-start.3 = (bf16[1,2,96,416]{3,0,2,1:T(2,128)(2,1)S(1)}, bf16[1,2,96,416]{3,0,2,1:T(2,128)(2,1)S(1)}, u32[]{:S(2)}, u32[]{:S(2)}) collective-permute-start(bf16[1,2,96,416]{3,0,2,1:T(2,128)(2,1)S(1)} %copy.129), channel_id=1, source_target_pairs={{4,0},{8,4},{12,8},{16,12},{20,16},{24,20},{28,24},{0,28},{5,1},{9... | collective-permute-start | bytes 479240 | tf_op jit(solution)/shard_map/ppermute | solution.py:13
  21.7 12.7 %psum.7 = f32[2,1,1,416]{3,0,2,1:T(2,128)S(1)} all-reduce(f32[2,1,1,416]{3,0,2,1:T(2,128)S(1)} %bitcast.336), channel_id=1, replica_groups=mesh['req'=8,'mp'=4] {'mp'}, use_global_device_ids=true, to_apply=%region_3.4 | all-reduce | flops 832 | bytes 6656 | tf_op jit(solution)/shard_map/psum | solution.py:99
  36.3 1.5 convolution_convert_fusion
  37.8 1.7 %pad_maximum_fusion.2 = bf16[2,3,96,416]{3,0,2,1:T(2,128)(2,1)} fusion(bf16[2,1,96,416]{3,0,2,1:T(2,128)(2,1)S(1)} %copy.131, bf16[2,2,96,416]{3,0,2,1:T(2,128)(2,1)S(1)} %convolution_convert_fusion), kind=kLoop, calls=%fused_computation.110 | loop fusion | flops 239616 | bytes 958464 | tf_op jit(solution)/shard_map/concatenate | solution.py:101
  40.2 0.6 fusion.49
  40.8 0.8 copy.160
  41.6 45.3 %all-gather.2.cloned.1.call-done = bf16[2,3,384,416]{3,0,2,1:T(2,128)(2,1)} async-done(((bf16[2,3,96,416]{3,0,2,1:T(2,128)(2,1)}), bf16[2,3,384,416]{3,0,2,1:T(2,128)(2,1)}) %all-gather.2.cloned.1.call-update) | async-done | bytes 1916944 | tf_op jit(solution)/shard_map/all_gather | solution.py:103
  87.0 18.8 %slice_multiply_fusion.2 = (bf16[2,3,384,624]{3,0,2,1:T(2,128)(2,1)S(1)}, bf16[2,3,384,624]{3,0,2,1:T(2,128)(2,1)S(1)}, bf16[2,3,384,624]{3,0,2,1:T(2,128)(2,1)S(1)}) fusion(bf16[624]{0:T(1024)(128)(2,1)S(1)} %fusion.127, bf16[2,3,384,416]{3,0,2,1:T(2,128)(2,1)} %all-gather.2.cloned.1.call-done, bf16[624]{0:T(1024)(128)(2,1)S(1)} %fusion.129, ...), kind=kLoop, calls=%fused_computation.2 | loop fusion | flops 17252352 | bytes 10546848 | tf_op jit(solution)/shard_map/mul | solution.py:25
  105.8 10.7 %slice_bitcast_fusion.18 = (bf16[2,384,416]{2,0,1:T(2,128)(2,1)S(1)}, bf16[2,384,416]{2,0,1:T(2,128)(2,1)S(1)}, bf16[2,384,416]{2,0,1:T(2,128)(2,1)S(1)}, bf16[2...) fusion(bf16[2,3,384,624]{3,0,2,1:T(2,128)(2,1)S(1)} %get-tuple-, ...), kind=kLoop, calls=%fused_computation.66 | loop fusion | bytes 11501568 | tf_op jit(solution)/shard_map/reshape.33
  116.8 25.4 %slice_bitcast_fusion.8 = (bf16[2,384,416]{2,0,1:T(2,128)(2,1)S(1)}, bf16[2,384,416]{2,0,1:T(2,128)(2,1)S(1)}, bf16[2,384,416]{2,0,1:T(2,128)(2,1)S(1)}, bf16[2,...) fusion(bf16[2,3,384,624]{3,0,2,1:T(2,128)(2,1)S(1)} %get-tuple-, ...), kind=kLoop, calls=%fused_computation.56 | loop fusion | bytes 23003136 | tf_op jit(solution)/shard_map/reshape.53
  147.7 0.3 convolution_add_fusion.5
  148.0 0.3 convolution_add_fusion.4
  148.3 0.3 convolution_add_fusion.3
  148.6 0.3 convolution_add_fusion.2
  149.6 1.1 fusion.17
  (52 shorter events, 7.5 us)
Async XLA Ops:
  7.2 79.8 %all-gather.2.cloned.1.call-start = ((), (), s32[]{:S(2)}) async-start(), calls=%async_computation | async-start | bytes 2949120 | tf_op jit(solution)/shard_map/all_gather | solution.py:103
  9.5 25.4 %collective-permute-start = (bf16[1]{0:T(256)(128)(2,1)}, bf16[1]{0:T(256)(128)(2,1)}, u32[]{:S(2)}, u32[]{:S(2)}) collective-permute-start(bf16[1]{0:T(256)(128)(2,1)} %bitcast.4), channel_id=1, source_target_pairs={{28,0},{0,4},{4,8},{8,12},{12,16},{16,20},{20,24},{24,28},{29,1},{... | collective-permute-start | bytes 14 | tf_op jit(solution)/shard_map/ppermute | solution.py:13
  11.7 23.9 %collective-permute-start.1 = (bf16[1]{0:T(256)(128)(2,1)}, bf16[1]{0:T(256)(128)(2,1)}, u32[]{:S(2)}, u32[]{:S(2)}) collective-permute-start(bf16[1]{0:T(256)(128)(2,1)} %bitcast.7), channel_id=1, source_target_pairs={{4,0},{8,4},{12,8},{16,12},{20,16},{24,20},{28,24},{0,28},{5,1},{9... | collective-permute-start | bytes 14 | tf_op jit(solution)/shard_map/ppermute | solution.py:13
  17.6 4.0 %copy-start.3 = (bf16[96]{0:T(256)(128)(2,1)S(1)}, bf16[96]{0:T(256)(128)(2,1)}, u32[]{:S(2)}) copy-start(bf16[96]{0:T(256)(128)(2,1)} %param.11) | copy-start | bytes 580
  17.6 4.0 %copy-start.1 = (bf16[2,1,96,416]{3,2,1,0:T(8,128)(2,1)S(1)}, bf16[2,1,96,416]{3,2,1,0:T(8,128)(2,1)}, u32[]{:S(2)}) copy-start(bf16[2,1,96,416]{3,2,1,0:T(8,128)(2,1)} %param.7) | copy-start | bytes 479236
  18.0 18.3 %collective-permute-start.2 = (bf16[1,2,96,416]{3,0,2,1:T(2,128)(2,1)S(1)}, bf16[1,2,96,416]{3,0,2,1:T(2,128)(2,1)S(1)}, u32[]{:S(2)}, u32[]{:S(2)}) collective-permute-start(bf16[1,2,96,416]{3,0,2,1:T(2,128)(2,1)S(1)} %copy.128), channel_id=1, source_target_pairs={{28,0},{0,4},{4,8},{8,12},{12,16},{16,20},{20,24},{24,28},{29,1},{... | collective-permute-start | bytes 479240 | tf_op jit(solution)/shard_map/ppermute | solution.py:13
  19.0 17.3 %collective-permute-start.3 = (bf16[1,2,96,416]{3,0,2,1:T(2,128)(2,1)S(1)}, bf16[1,2,96,416]{3,0,2,1:T(2,128)(2,1)S(1)}, u32[]{:S(2)}, u32[]{:S(2)}) collective-permute-start(bf16[1,2,96,416]{3,0,2,1:T(2,128)(2,1)S(1)} %copy.129), channel_id=1, source_target_pairs={{4,0},{8,4},{12,8},{16,12},{20,16},{24,20},{28,24},{0,28},{5,1},{9... | collective-permute-start | bytes 479240 | tf_op jit(solution)/shard_map/ppermute | solution.py:13
  105.8 10.7 %copy-start = (bf16[27,96,384]{2,1,0:T(8,128)(2,1)S(1)}, bf16[27,96,384]{2,1,0:T(8,128)(2,1)}, u32[]{:S(2)}) copy-start(bf16[27,96,384]{2,1,0:T(8,128)(2,1)} %param.12) | copy-start | bytes 5971972
  148.9 0.7 copy-start.2
Sparse Core Ops, SparseCore 0:
  39.7 47.2 all-gather.1
where the time goes:
time: 158 us
  waiting for transfers between devices  45.3 us (29%)
  local copies, waits for them, and re-layouts  39.2 us (25%)
  other arithmetic  23.1 us (15%)
  between operations  17.7 us (11%)
  blocking collectives  12.7 us (8%)
  matrix products  11.2 us (7%)
  starting transfers between devices  8.27 us (5%)
    all_gather x1, waiting for transfers between devices, shards(): lax.all_gather(extended, 'mp', axis=2, tiled=True)  45.3 us
    another operation x2, local copies, waits for them, and re-layouts  36.1 us
    mul x1, other arithmetic, apply_taps(): shifted = padded[:, :, :, step_x:step_x + pixels + 2 * row_width] * inside  18.8 us
    psum x1, blocking collectives, shards(): squares = lax.psum(partial_squares, 'mp')  12.7 us
    dot_general x27, matrix products, apply_taps(): jnp.einsum('oc,stcp->stop', weights[step_t * 9 + step_y * 3 + step_x], wi...  8.54 us
    ppermute x4, starting transfers between devices, shifted_2(): return lax.ppermute(block, axis, route)  8.23 us
  transfers between devices with their start and end apart: 5, of which 1 were waited for; matrix products, arithmetic and copies ran while one was open for 3% of the time, Pallas kernels for 0%

commit v1 on v0

--- a/solution.py
+++ b/solution.py
@@ -2,9 +2,35 @@
 import jax.numpy as jnp
 from jax import lax
 from jax.sharding import PartitionSpec as P
+from jax.lax import axis_index, axis_size, ppermute
 
 SECTION_CHANNELS = 384
 LATENT_COLUMNS = 104
+
+
+def hold_the_spans(field_in, axis_k):
+    field_in = jnp.moveaxis(field_in, 0, axis_k)
+    outcome_arr = field_in.shape
+    return field_in.reshape(
+        *outcome_arr[:axis_k],
+        outcome_arr[axis_k] * outcome_arr[axis_k + 1],
+        *outcome_arr[axis_k + 2 :]
+    )
+
+
+def compute_the_digits(sheet, group_axis):
+    axis_len = axis_size(group_axis)
+    block_out = sheet[None]
+    for j in range(axis_len.bit_length() - 1):
+        r_now = 1 << j
+        trail = []
+        for u in [*range(axis_len)]:
+            trail.append((u, u ^ r_now))
+        val = ppermute(block_out, axis_name=group_axis, perm=trail)
+        shaped = jnp.stack([block_out, val], axis=0)
+        lower = axis_index(group_axis) >> j & 1
+        block_out = jnp.where(lower == 0, shaped, shaped[::-1]).reshape(-1, *sheet.shape)
+    return block_out
 
 
 def shifted_2(block, axis, distance):
@@ -99,8 +125,12 @@
     squares = lax.psum(partial_squares, "mp")
     hidden = normalize(latents, squares, norm_gain)
     extended = jnp.concatenate([moved, hidden], axis=1)
+
+    def point_circles_by_axis(base_x, buf, out_dim):
+        return hold_the_spans(compute_the_digits(base_x, buf), out_dim)
+
     conv_sum = apply_taps(
-        start_zero, lax.all_gather(extended, "mp", axis=2, tiled=True), conv_weight, LATENT_COLUMNS
+        start_zero, point_circles_by_axis(extended, "mp", out_dim=2), conv_weight, LATENT_COLUMNS
     )
     total = latents.astype(jnp.float32) + conv_sum + conv_bias[:, None]
     decoded = jnp.where(live, total, jnp.zeros_like(total)).astype(jnp.bfloat16)

time: 158 us -> 126 us (0.80); the launches traced: 158 us -> 124 us
  local copies, waits for them, and re-layouts: 39.2 us -> 5.95 us
  between operations: 17.7 us -> 4.16 us
  waiting for transfers between devices: 45.3 us -> 57.7 us
  other arithmetic: 23.1 us -> 21 us
  matrix products: 11.2 us -> 12.8 us
    ppermute x0 -> x2, waiting for transfers between devices: none -> 57.7 us  [compute_the_digits(): val = ppermute(block_out, axis_name=group_axis, perm=trail)]
    all_gather x1 -> x0, waiting for transfers between devices: 45.3 us -> none  [shards(): lax.all_gather(extended, 'mp', axis=2, tiled=True)]
    another operation x2 -> x0, local copies, waits for them, and re-layouts: 36.1 us -> none
    mul x1, other arithmetic: 18.8 us -> 5.69 us  [apply_taps(): shifted = padded[:, :, :, step_x:step_x + pixels + 2 * row_width] * inside]
    another operation x3 -> x7, other arithmetic: 0.35 us -> 10.5 us  [the longest x4 10.1 us: compute_the_digits(): shaped = jnp.stack([block_out, val], axis=0)]
    reshape x0 -> x2, local copies, waits for them, and re-layouts: none -> 2.86 us  [the longest x1 2.37 us: hold_the_spans(): field_in.reshape(*outcome_arr[:axis_k], outcome_arr[axis_k] * outcome_arr...]
    select_n x0 -> x1, other arithmetic: none -> 2.54 us  [compute_the_digits(): jnp.where(lower == 0, shaped, shaped[::-1]).reshape(-1, *sheet.shape)]
    concatenate x2 -> x1, other arithmetic: 2.28 us -> 0.59 us  [shards(): extended = jnp.concatenate([moved, hidden], axis=1)]
  transfers between devices with their start and end apart: 5 -> 6, of which waited for: 1 -> 2; matrix products, arithmetic and copies ran while one was open for 3% -> 4% of each run, Pallas kernels for 0% -> 0%
where the time goes in v1:
time: 126 us; the launch traced here: 124 us
  waiting for transfers between devices  57.7 us (46%)
  other arithmetic  21 us (17%)
  matrix products  12.8 us (10%)
  blocking collectives  12.7 us (10%)
  starting transfers between devices  9.49 us (8%)
  local copies, waits for them, and re-layouts  5.95 us (5%)
  between operations  4.16 us (3%)
    ppermute x2, waiting for transfers between devices, compute_the_digits(): val = ppermute(block_out, axis_name=group_axis, perm=trail)  57.7 us
    psum x1, blocking collectives, shards(): squares = lax.psum(partial_squares, 'mp')  12.7 us
    dot_general x27, matrix products, apply_taps(): jnp.einsum('oc,stcp->stop', weights[step_t * 9 + step_y * 3 + step_x], wi...  10.2 us
    another operation x4, other arithmetic, compute_the_digits(): shaped = jnp.stack([block_out, val], axis=0)  10.1 us
    ppermute x4, starting transfers between devices, shifted_2(): return lax.ppermute(block, axis, route)  8.23 us
    mul x1, other arithmetic, apply_taps(): shifted = padded[:, :, :, step_x:step_x + pixels + 2 * row_width] * inside  5.69 us
    select_n x1, other arithmetic, compute_the_digits(): jnp.where(lower == 0, shaped, shaped[::-1]).reshape(-1, *sheet.shape)  2.54 us
  transfers between devices with their start and end apart: 6, of which 2 were waited for; matrix products, arithmetic and copies ran while one was open for 4% of the time, Pallas kernels for 0%

profile of v1, /device:TPU:0, one launch (start us, length us, event | category | flops | bytes accessed | tf_op | source)
XLA Modules:
  0.0 123.9 jit_solution(8398442726041553217)
XLA Ops:
  0.6 0.7 fusion.118
  1.7 0.6 select_reduce_fusion.1
  2.9 1.5 %collective-permute-start = (bf16[1]{0:T(256)(128)(2,1)}, bf16[1]{0:T(256)(128)(2,1)}, u32[]{:S(2)}, u32[]{:S(2)}) collective-permute-start(bf16[1]{0:T(256)(128)(2,1)} %bitcast.4), channel_id=1, source_target_pairs={{28,0},{0,4},{4,8},{8,12},{12,16},{16,20},{20,24},{24,28},{29,1},{... | collective-permute-start | bytes 14 | tf_op jit(solution)/shard_map/ppermute | solution.py:39
  5.1 4.0 %collective-permute-start.1 = (bf16[1]{0:T(256)(128)(2,1)}, bf16[1]{0:T(256)(128)(2,1)}, u32[]{:S(2)}, u32[]{:S(2)}) collective-permute-start(bf16[1]{0:T(256)(128)(2,1)} %bitcast.7), channel_id=1, source_target_pairs={{4,0},{8,4},{12,8},{16,12},{20,16},{24,20},{28,24},{0,28},{5,1},{9... | collective-permute-start | bytes 14 | tf_op jit(solution)/shard_map/ppermute | solution.py:39
  9.1 1.4 %copy.79 = bf16[2,2,96,416]{3,0,2,1:T(2,128)(2,1)S(1)} copy(bf16[2,2,96,416]{3,2,1,0:T(8,128)(2,1)} %param.8) | data formatting | bytes 638976 | tf_op args[1]
  10.5 0.6 fusion.113
  11.5 0.6 fusion.111
  12.4 2.7 %collective-permute-start.3 = (bf16[1,2,96,416]{3,0,2,1:T(2,128)(2,1)S(1)}, bf16[1,2,96,416]{3,0,2,1:T(2,128)(2,1)S(1)}, u32[]{:S(2)}, u32[]{:S(2)}) collective-permute-start(bf16[1,2,96,416]{3,0,2,1:T(2,128)(2,1)S(1)} %copy.78), channel_id=1, source_target_pairs={{4,0},{8,4},{12,8},{16,12},{20,16},{24,20},{28,24},{0,28},{5,1},{9... | collective-permute-start | bytes 479240 | tf_op jit(solution)/shard_map/ppermute | solution.py:39
  15.2 12.7 %psum.7 = f32[2,1,1,416]{3,0,2,1:T(2,128)S(1)} all-reduce(f32[2,1,1,416]{3,0,2,1:T(2,128)S(1)} %bitcast.380), channel_id=1, replica_groups=mesh['req'=8,'mp'=4] {'mp'}, use_global_device_ids=true, to_apply=%region_3.4 | all-reduce | flops 832 | bytes 6656 | tf_op jit(solution)/shard_map/psum | solution.py:125
  29.7 1.5 %convolution_convert_fusion = bf16[2,2,96,416]{3,0,2,1:T(2,128)(2,1)S(1)} fusion(bf16[1,2,96,416]{3,0,2,1:T(2,128)(2,1)S(1)} %collective-permute-done.3, bf16[1,2,96,416]{3,0,2,1:T(2,128)(2,1)S(1)} %collective-permute-done.2, bf16[2,2,96,416]{3,0,2,1:T(2,128)(2,1)S(1)} %copy.79, f32[4]{0:T(128)S(1)} %pad_maximum_fusion.5), kind=kOutput, calls=%fused_computation.9 | convolution fusion | flops 3354632 | bytes 958480 | tf_op jit(solution)/shard_map/ns,sfkp->nfkp/dot_general | solution.py:101
  31.2 1.0 fusion.123
  32.3 11.3 %collective-permute-done.4 = bf16[1,2,3,96,416]{4,1,3,2,0:T(2,128)(2,1)S(1)} collective-permute-done((bf16[1,2,3,96,416]{4,1,3,2,0:T(2,128)(2,1)S(1)}, bf16[1,2,3,96,416]{4,1,3,2,0:T(2,128)(2,1)S(1)}, u32[]{:S(2)}, u32[]{:S(2)}) %collective-permute-start.4) | collective-permute-done | bytes 479264 | tf_op jit(solution)/shard_map/ppermute | solution.py:29
  43.6 1.8 %pad_maximum_fusion.1 = bf16[2,1,2,3,96,416]{5,2,4,3,1,0:T(2,128)(2,1)S(1)} fusion(bf16[1,1,2,3,96,416]{5,2,4,3,1,0:T(2,128)(2,1)S(1)} %bitcast.379, bf16[1,1,2,3,96,416]{5,2,4,3,1,0:T(2,128)(2,1)S(1)} %get-tuple-element.18), kind=kLoop, calls=%fused_computation.52 | loop fusion | flops 479232 | bytes 1916928 | tf_op jit(solution)/shard_map/stack | solution.py:30
  45.4 2.6 %fusion.91 = (bf16[1,2,2,3,96,416]{5,2,4,3,1,0:T(2,128)(2,1)S(1)}, bf16[2,2,3,96,416]{4,1,3,2,0:T(2,128)(2,1)}) fusion(bf16[2,1,2,3,96,416]{5,2,4,3,1,0:T(2,128)(2,1)S(1)} %pad_maximum_fusion.1, pred[]{:T(512)S(6)} %eq.48), kind=kLoop, calls=%fused_computation.160 | loop fusion | flops 479232 | bytes 2875393 | tf_op jit(solution)/shard_map/stack;reshape | solution.py:30
  48.0 1.2 collective-permute-start.5
  49.9 0.6 fusion.25
  50.5 0.8 copy.84
  51.3 46.4 %collective-permute-done.5 = bf16[2,2,3,96,416]{4,1,3,2,0:T(2,128)(2,1)} collective-permute-done((bf16[2,2,3,96,416]{4,1,3,2,0:T(2,128)(2,1)}, bf16[2,2,3,96,416]{4,1,3,2,0:T(2,128)(2,1)}, u32[]{:S(2)}, u32[]{:S(2)}) %collective-permute-start.5) | collective-permute-done | bytes 958496 | tf_op jit(solution)/shard_map/ppermute | solution.py:29
  97.7 4.8 %pad_maximum_fusion = bf16[2,2,2,3,96,416]{5,2,4,3,1,0:T(2,128)(2,1)S(1)} fusion(bf16[1,2,2,3,96,416]{5,2,4,3,1,0:T(2,128)(2,1)} %bitcast.25, bf16[1,2,2,3,96,416]{5,2,4,3,1,0:T(2,128)(2,1)S(1)} %get-tuple-element.16), kind=kLoop, calls=%fused_computation.7 | loop fusion | flops 958464 | bytes 3833856 | tf_op jit(solution)/shard_map/stack | solution.py:30
  102.5 2.5 %broadcast_select_fusion = bf16[2,2,2,3,96,416]{5,2,4,3,1,0:T(2,128)(2,1)S(1)} fusion(bf16[2,2,2,3,96,416]{5,2,4,3,1,0:T(2,128)(2,1)S(1)} %pad_maximum_fusion, pred[]{:T(512)S(6)} %eq.47), kind=kLoop, calls=%fused_computation | loop fusion | flops 958464 | bytes 3833857 | tf_op jit(solution)/shard_map/jit(_where)/select_n | solution.py:32
  105.0 0.5 copy.81
  105.5 2.4 %copy.82 = bf16[2,3,384,416]{2,3,0,1:T(8,128)(2,1)} copy(bf16[2,3,384,416]{3,2,1,0:T(8,128)(2,1)S(1)} %bitcast.378) | data formatting | bytes 3833856 | tf_op jit(solution)/shard_map/reshape | solution.py:14
  107.9 5.7 %fusion = (bf16[2,3,384,624]{2,3,0,1:T(8,128)(2,1)S(1)}, bf16[2,3,384,624]{2,3,0,1:T(8,128)(2,1)S(1)}, bf16[2,3,384,624]{2,3,0,1:T(8,128)(2,1)S(1)}) fusion(bf16[2,3,384,416]{2,3,0,1:T(8,128)(2,1)} %copy.82, bf16[624]{0:T(1024)(128)(2,1)S(1)} %get-tuple-element.23, bf16[624]{0:T(1024)(128)(2,1)S(1)} %fusion.107, bf16[624]{0:T(1024)(128)(2,1)S(1)} %get-tuple-element.22), kind=kLoop, calls=%fused_computation.4 | loop fusion | flops 17252352 | bytes 10546848 | tf_op jit(solution)/shard_map/mul | solution.py:51
  122.7 1.2 fusion.20
  (56 shorter events, 10.8 us)
Async XLA Ops:
  2.9 25.4 %collective-permute-start = (bf16[1]{0:T(256)(128)(2,1)}, bf16[1]{0:T(256)(128)(2,1)}, u32[]{:S(2)}, u32[]{:S(2)}) collective-permute-start(bf16[1]{0:T(256)(128)(2,1)} %bitcast.4), channel_id=1, source_target_pairs={{28,0},{0,4},{4,8},{8,12},{12,16},{16,20},{20,24},{24,28},{29,1},{... | collective-permute-start | bytes 14 | tf_op jit(solution)/shard_map/ppermute | solution.py:39
  5.1 23.9 %collective-permute-start.1 = (bf16[1]{0:T(256)(128)(2,1)}, bf16[1]{0:T(256)(128)(2,1)}, u32[]{:S(2)}, u32[]{:S(2)}) collective-permute-start(bf16[1]{0:T(256)(128)(2,1)} %bitcast.7), channel_id=1, source_target_pairs={{4,0},{8,4},{12,8},{16,12},{20,16},{24,20},{28,24},{0,28},{5,1},{9... | collective-permute-start | bytes 14 | tf_op jit(solution)/shard_map/ppermute | solution.py:39
  10.5 4.6 %copy-start.3 = (bf16[96]{0:T(256)(128)(2,1)S(1)}, bf16[96]{0:T(256)(128)(2,1)}, u32[]{:S(2)}) copy-start(bf16[96]{0:T(256)(128)(2,1)} %param.11) | copy-start | bytes 580
  10.5 4.6 %copy-start.1 = (bf16[2,1,96,416]{3,2,1,0:T(8,128)(2,1)S(1)}, bf16[2,1,96,416]{3,2,1,0:T(8,128)(2,1)}, u32[]{:S(2)}) copy-start(bf16[2,1,96,416]{3,2,1,0:T(8,128)(2,1)} %param.7) | copy-start | bytes 479236
  11.4 18.3 %collective-permute-start.2 = (bf16[1,2,96,416]{3,0,2,1:T(2,128)(2,1)S(1)}, bf16[1,2,96,416]{3,0,2,1:T(2,128)(2,1)S(1)}, u32[]{:S(2)}, u32[]{:S(2)}) collective-permute-start(bf16[1,2,96,416]{3,0,2,1:T(2,128)(2,1)S(1)} %copy.77), channel_id=1, source_target_pairs={{28,0},{0,4},{4,8},{8,12},{12,16},{16,20},{20,24},{24,28},{29,1},{... | collective-permute-start | bytes 479240 | tf_op jit(solution)/shard_map/ppermute | solution.py:39
  12.4 17.3 %collective-permute-start.3 = (bf16[1,2,96,416]{3,0,2,1:T(2,128)(2,1)S(1)}, bf16[1,2,96,416]{3,0,2,1:T(2,128)(2,1)S(1)}, u32[]{:S(2)}, u32[]{:S(2)}) collective-permute-start(bf16[1,2,96,416]{3,0,2,1:T(2,128)(2,1)S(1)} %copy.78), channel_id=1, source_target_pairs={{4,0},{8,4},{12,8},{16,12},{20,16},{24,20},{28,24},{0,28},{5,1},{9... | collective-permute-start | bytes 479240 | tf_op jit(solution)/shard_map/ppermute | solution.py:39
  32.2 11.4 %collective-permute-start.4 = (bf16[1,2,3,96,416]{4,1,3,2,0:T(2,128)(2,1)S(1)}, bf16[1,2,3,96,416]{4,1,3,2,0:T(2,128)(2,1)S(1)}, u32[]{:S(2)}, u32[]{:S(2)}) collective-permute-start(bf16[1,2,3,96,416]{4,1,3,2,0:T(2,128)(2,1)S(1)} %get-tuple-element.19), channel_id=1, source_target_pairs={{0,1},{1,0},{2,3},{3,2},{4,5},{5,4},{6,7},{7,6},{8,9},{9,8},{10,11... | collective-permute-start | bytes 1437704 | tf_op jit(solution)/shard_map/ppermute | solution.py:29
  48.0 49.7 %collective-permute-start.5 = (bf16[2,2,3,96,416]{4,1,3,2,0:T(2,128)(2,1)}, bf16[2,2,3,96,416]{4,1,3,2,0:T(2,128)(2,1)}, u32[]{:S(2)}, u32[]{:S(2)}) collective-permute-start(bf16[2,2,3,96,416]{4,1,3,2,0:T(2,128)(2,1)} %get-tuple-element.17), channel_id=1, source_target_pairs={{0,2},{1,3},{2,0},{3,1},{4,6},{5,7},{6,4},{7,5},{8,10},{9,11},{10,... | collective-permute-start | bytes 2875400 | tf_op jit(solution)/shard_map/ppermute | solution.py:29
  107.9 5.7 %copy-start = (bf16[27,96,384]{2,1,0:T(8,128)(2,1)S(1)}, bf16[27,96,384]{2,1,0:T(8,128)(2,1)}, u32[]{:S(2)}) copy-start(bf16[27,96,384]{2,1,0:T(8,128)(2,1)} %param.12) | copy-start | bytes 5971972
  121.6 1.1 copy-start.2
